TPU v7x, 32 devices: a whole 2x2x4 slice. The times are simulated.
32 devices in a mesh: wide: 8 (over z, y), lev: 4 (over x, core).
Axes of the slice: x: 2, y: 2, z: 4, core: 2. Of those that a mesh axis runs over, the one named last changes fastest.
Arguments:
- state_field: float32 [12, 1472, 1472], P('lev', 'wide'), may hold values from -8 to 8
- to_modes: float32 [12, 12], replicated, may hold values from -4 to 4
- from_modes: float32 [12, 12], replicated, may hold values from -4 to 4, as said below
- mode_depth: float32 [12], replicated, may hold values from 0.1 to 2000
Outputs:
- updated_field: float32 [12, 1472, 1472], P('lev', 'wide')
Inputs may be any that keep to these rules, and one draw needn't show every extreme that they name: `from_modes`: the inverse of to_modes.
All inputs are finite; a program needn't handle non-finite values.
Results may differ from a plain program's by a relative error of at most 0.000094.
Values sent between devices are 32-bit elements; how exact they have to be, the bound alone decides.
No kernel may reach another device: no remote copies, remote signals or barrier semaphores. Data moves between devices by JAX's collectives and lax.ppermute only.
A program may use at most 64 MiB of HBM per device.

v0:
```python
import math
import jax
import jax.numpy as jnp
from jax import lax
from jax.sharding import PartitionSpec as P

I = 1472
E = 64
KT = 512
highest = lax.Precision.HIGHEST


def spread(block, axis, owner):
    block = jnp.where(lax.axis_index(axis) == owner, block, jnp.zeros_like(block))
    return lax.psum(block, axis)


def blend_weights(fraction):
    square = fraction * fraction
    cubed = square * fraction
    return (
        2.0 * cubed - 3.0 * square + 1.0,
        cubed - 2.0 * square + fraction,
        -2.0 * cubed + 3.0 * square,
        cubed - square,
    )


def hermite_mix(start_val, start_slope, end_val, end_slope, weights):
    return (
        weights[0] * end_val
        + weights[1] * end_slope
        + weights[2] * start_val
        + weights[3] * start_slope
    )


def extend_cols(sub_block, extra):
    fraction = (jnp.arange(extra, dtype=jnp.float32) + 1.0) / (extra + 1.0)
    weights = blend_weights(fraction)
    end_val = sub_block[..., -1:]
    end_slope = sub_block[..., -1:] - sub_block[..., -2:-1]
    start_val = sub_block[..., :1]
    start_slope = sub_block[..., 1:2] - sub_block[..., :1]
    added = hermite_mix(start_val, start_slope, end_val, end_slope, weights)
    return jnp.concatenate([sub_block, added], axis=-1)


def laplace(waves, length):
    sines = jnp.sin(math.pi / length * waves.astype(jnp.float32))
    return 4.0 * sines * sines


def cas_table(positions, waves, length):
    product = positions[:, None] * waves[None, :] % length
    phase_angle = 2.0 * math.pi / length * product.astype(jnp.float32)
    return jnp.cos(phase_angle) + jnp.sin(phase_angle)


def wave_numbers(amount, length, bound):
    indices = jnp.arange(amount, dtype=jnp.int32)
    waves = jnp.where(indices < bound, indices, length - 2 * bound + 1 + indices)
    live_mask = indices < 2 * bound - 1
    waves = jnp.where(live_mask, waves, 0)
    magnitude = jnp.minimum(waves, length - waves)
    return (waves, live_mask.astype(jnp.float32), magnitude)


def shards(state_field, to_modes, from_modes, mode_depth):
    wide_count = lax.axis_size("wide")
    wide_index = lax.axis_index("wide")
    lev_index = lax.axis_index("lev")
    levels, row_count, col_count = state_field.shape
    length = I + E
    ext_count = E // wide_count
    row_total = row_count + ext_count
    head_strip = spread(state_field[:, :2], "wide", 0)
    tail_strip = spread(state_field[:, row_count - 2 :], "wide", wide_count - 1)
    ext_slot = (wide_count - wide_index) % wide_count
    row_ids = ext_slot * ext_count + jnp.arange(ext_count, dtype=jnp.int32)
    fraction = (row_ids.astype(jnp.float32) + 1.0) / (E + 1.0)
    weights = tuple((weight[:, None] for weight in blend_weights(fraction)))
    end_val = tail_strip[:, 1:2]
    end_slope = tail_strip[:, 1:2] - tail_strip[:, 0:1]
    start_val = head_strip[:, 0:1]
    start_slope = head_strip[:, 1:2] - head_strip[:, 0:1]
    ext_block = hermite_mix(start_val, start_slope, end_val, end_slope, weights)
    stacked = jnp.concatenate([state_field, ext_block], axis=1)
    widened = extend_cols(stacked, E)
    spec_count = 2 * KT
    waves, live_mask, magnitude = wave_numbers(spec_count, length, KT)
    lap_all = laplace(waves, length)
    positions = jnp.arange(length, dtype=jnp.int32)
    forward_x = cas_table(positions, waves, length) * live_mask[None, :]
    row_owner = positions // row_total
    local_row = positions % row_total
    ext_owner = (wide_count - row_owner) % wide_count
    row_pos = jnp.where(
        local_row < row_count,
        row_owner * row_count + local_row,
        I + ext_owner * ext_count + local_row - row_count,
    )
    forward_y = cas_table(row_pos, waves, length) * live_mask[None, :]
    inverse_y = forward_y.T / length
    inverse_x = forward_x[:I].T / length
    col_span = spec_count // wide_count
    col_start = wide_index * col_span
    spec_x = jnp.einsum("irn,nc->irc", widened, forward_x, precision=highest)
    spectrum = jnp.einsum(
        "irc,rk->ick",
        lax.all_to_all(spec_x, "wide", split_axis=2, concat_axis=1, tiled=True),
        forward_y,
        precision=highest,
    )
    lev_start = lev_index * levels
    sub_block = lax.dynamic_slice(to_modes, (0, lev_start), (lax.axis_size("lev") * levels, levels))
    mode_values = lax.psum_scatter(
        jnp.einsum("ml,lck->mck", sub_block, spectrum, precision=highest),
        "lev",
        scatter_dimension=0,
        tiled=True,
    )
    lap_cols = lax.dynamic_slice_in_dim(lap_all, col_start, col_span)
    mag_cols = lax.dynamic_slice_in_dim(magnitude, col_start, col_span)
    live_cols = lax.dynamic_slice_in_dim(live_mask, col_start, col_span)
    inside = (
        mag_cols[:, None] * mag_cols[:, None] + magnitude[None, :] * magnitude[None, :] < KT * KT
    )
    keep_mask = live_cols[:, None] * live_mask[None, :] * inside.astype(jnp.float32)
    keep_mask, lap_sum = (keep_mask, lap_cols[:, None] + lap_all[None, :])
    mode_rates = lax.dynamic_slice_in_dim(mode_depth, lev_start, levels)
    solved = mode_values * keep_mask / (1.0 + mode_rates[:, None, None] * lap_sum)
    shard_piece = lax.all_gather(solved, "lev", axis=0, tiled=True)
    sub_block = lax.dynamic_slice(from_modes, (lev_start, 0), (levels, shard_piece.shape[0]))
    mixed_levels = jnp.einsum("lm,mck->lck", sub_block, shard_piece, precision=highest)
    rows_back = jnp.einsum("ick,kr->icr", mixed_levels, inverse_y, precision=highest)
    return jnp.einsum(
        "icr,cn->irn",
        lax.all_to_all(rows_back, "wide", split_axis=2, concat_axis=1, tiled=True)[
            :, :, :row_count
        ],
        inverse_x,
        precision=highest,
    )


def solution(mesh):
    placed = (P("lev", "wide", None), P(), P(), P())
    return jax.shard_map(
        shards, mesh=mesh, in_specs=placed, out_specs=P("lev", "wide", None), check_vma=False
    )
```

profile of v0, /device:TPU:0, one launch (start us, length us, event | category | flops | bytes accessed | tf_op | source)
XLA Modules:
  0.0 513.1 jit_solution(13678874333688489325)
XLA Ops:
  6.5 0.0 copy-start
  6.5 0.0 copy-start.4
  6.5 0.0 all-reduce.3.cloned.1.call-start
  6.5 1.8 slice_select_fusion.1
  8.3 0.0 all-reduce.3.cloned.1.call-update
  8.5 74.6 %all-reduce.3.cloned.1.call-done = (f32[3,2,1472]{2,1,0:T(2,128)}, f32[3,2,1472]{2,1,0:T(2,128)}) async-done(((f32[3,2,1472]{2,1,0:T(2,128)}, f32[3,2,1472]{2,1,0:T(2,128)}), (f32[3,2,1472]{2,1,0:T(2,128)}, f32[3,2,1472]{2,1,0:T(2,128)})) %all-reduce.3.cloned.1.call-update) | async-done | bytes 70672 | tf_op jit(solution)/shard_map/psum | solution.py:15
  83.1 0.9 fusion.107
  84.1 0.1 multiply_add_fusion.1
  84.2 2.0 fusion.66
  86.2 0.4 multiply_add_fusion
  86.6 0.0 copy-done.4
  86.6 0.4 fusion.124
  87.0 38.5 %fusion.12 = f32[3,192,1024]{2,1,0:T(8,128)S(1)} fusion(f32[1024]{0:T(1024)S(1)} %fusion.85, s32[1024]{0:T(1024)S(1)} %fusion.86, f32[3,192,1536]{2,1,0:T(8,128)S(1)} %fusion.124), kind=kOutput, calls=%fused_computation.15 | convolution fusion | flops 10888937472 | bytes 5906432 | tf_op jit(solution)/shard_map/irn,nc->irc/dot_general | solution.py:108
  125.5 3.2 copy.32
  128.7 4.8 all-to-all-start
  133.5 0.0 reduce-scatter.2.cloned.1.call-start
  133.5 91.4 %all-to-all-done = f32[3,192,1024]{1,0,2:T(4,128)} async-done(((f32[3,192,1024]{1,0,2:T(4,128)}), f32[3,192,1024]{1,0,2:T(4,128)}, u32[]{:S(2)}, u32[]{:S(2)}) %all-to-all-start) | async-done | bytes 2359328 | tf_op jit(solution)/shard_map/all_to_all | solution.py:111
  224.9 3.4 copy.45
  228.3 41.6 %fusion.10 = f32[3,128,1024]{2,1,0:T(8,128)S(1)} fusion(f32[3,1536,128]{2,1,0:T(8,128)S(1)} %bitcast.57, s32[1536]{0:T(1024)S(1)} %fusion.78, f32[1024]{0:T(1024)S(1)} %fusion.85, s32[1024]{0:T(1024)S(1)} %fusion.86), kind=kOutput, calls=%fused_computation.13 | convolution fusion | flops 7265058816 | bytes 3946496 | tf_op jit(solution)/shard_map/irc,rk->ick/dot_general | solution.py:109
  270.0 0.0 copy-done
  270.0 7.3 %fusion.59 = f32[12,128,1024]{2,0,1:T(8,128)S(1)} fusion(f32[3,128,1024]{2,1,0:T(8,128)S(1)} %fusion.10, f32[12,12]{1,0:T(8,128)S(1)} %copy-done, s32[]{:T(128)S(6)} %select_n.144), kind=kOutput, calls=%fused_computation.63 | convolution fusion | flops 56623104 | bytes 7864900 | tf_op jit(solution)/shard_map/ml,lck->mck/dot_general | solution.py:118
  277.3 6.3 %copy.37 = f32[12,128,1024]{2,1,0:T(8,128)} copy(f32[12,128,1024]{2,0,1:T(8,128)S(1)} %fusion.59) | data formatting | bytes 12582912 | tf_op jit(solution)/shard_map/ml,lck->mck/dot_general | solution.py:118
  283.6 0.0 copy-start.5
  283.6 0.0 reduce-scatter.2.cloned.1.call-update
  283.6 0.0 all-gather.2.cloned.1.call-start
  283.7 0.1 dynamic_slice.21
  283.8 0.1 dynamic_slice.23
  283.9 0.4 copy-done.5
  284.3 0.1 dynamic_slice.22
  284.3 0.1 dynamic-slice_multiply_fusion
  284.4 0.1 broadcast_add_fusion
  284.5 0.2 multiply_select_fusion
  284.7 56.9 %reduce-scatter.2.cloned.1.call-done = f32[3,128,1024]{2,1,0:T(8,128)} async-done(((f32[12,128,1024]{2,1,0:T(8,128)}), f32[3,128,1024]{2,1,0:T(8,128)}) %reduce-scatter.2.cloned.1.call-update) | async-done | bytes 1572880 | tf_op jit(solution)/shard_map/reduce_scatter | solution.py:117
  341.7 2.9 add_divide_fusion
  344.6 0.0 all-gather.2.cloned.1.call-update
  344.7 27.9 %fusion.122 = f32[1024,1536,1]{1,0,2:T(8,128)} fusion(f32[1024]{0:T(1024)S(1)} %fusion.85, s32[1024]{0:T(1024)S(1)} %fusion.86, s32[1536]{0:T(1024)S(1)} %fusion.78), kind=kLoop, calls=%fused_computation.12.clone.1 | loop fusion | flops 18874368 | bytes 6305792 | tf_op jit(solution)/shard_map/ick,kr->icr/dot_general | solution.py:136
  372.5 18.7 %all-gather.2.cloned.1.call-done = f32[12,128,1024]{2,1,0:T(8,128)} async-done(((f32[3,128,1024]{2,1,0:T(8,128)}), f32[12,128,1024]{2,1,0:T(8,128)}) %all-gather.2.cloned.1.call-update) | async-done | bytes 6291472 | tf_op jit(solution)/shard_map/all_gather | solution.py:133
  391.2 0.0 copy-start.2
  391.2 11.3 %fusion = f32[3,128,1024]{2,0,1:T(4,128)S(1)} fusion(f32[12,128,1024]{2,1,0:T(8,128)} %all-gather.2.cloned.1.call-done, f32[12,12]{1,0:T(8,128)} %param.6, s32[]{:T(128)S(6)} %select_n.144), kind=kOutput, calls=%fused_computation.3 | convolution fusion | flops 56623104 | bytes 7866372 | tf_op jit(solution)/shard_map/lm,mck->lck/dot_general | solution.py:135
  402.5 0.0 copy-done.2
  402.5 8.6 %fusion.8 = f32[3,128,1536]{2,1,0:T(8,128)S(1)} fusion(f32[3,128,1024]{2,0,1:T(4,128)S(1)} %fusion, f32[1024,1536,1]{1,0,2:T(8,128)S(1)} %copy-done.2), kind=kOutput, calls=%fused_computation.11 | convolution fusion | flops 7247757312 | bytes 10223616 | tf_op jit(solution)/shard_map/ick,kr->icr/dot_general | solution.py:136
  411.1 2.7 copy.40
  413.9 5.8 %all-to-all-start.1 = ((f32[3,128,1536]{1,0,2:T(4,128)}), f32[3,128,1536]{1,0,2:T(4,128)S(1)}, u32[]{:S(2)}, u32[]{:S(2)}) async-start(f32[3,128,1536]{1,0,2:T(4,128)} %copy.40), calls=%async_computation.2 | async-start | bytes 6291456 | tf_op jit(solution)/shard_map/all_to_all | solution.py:139
  419.6 27.2 %add_multiply_fusion = f32[1536,1024]{1,0:T(8,128)} fusion(f32[1024]{0:T(1024)S(1)} %fusion.85, s32[1024]{0:T(1024)S(1)} %fusion.86), kind=kLoop, calls=%fused_computation.32 | loop fusion | flops 17301504 | bytes 6299648 | tf_op jit(solution)/shard_map/mul | solution.py:94
  446.8 43.9 %all-to-all-done.1 = f32[3,128,1536]{1,0,2:T(4,128)S(1)} async-done(((f32[3,128,1536]{1,0,2:T(4,128)}), f32[3,128,1536]{1,0,2:T(4,128)S(1)}, u32[]{:S(2)}, u32[]{:S(2)}) %all-to-all-start.1) | async-done | bytes 2359328 | tf_op jit(solution)/shard_map/all_to_all | solution.py:139
  490.7 0.0 copy-start.3
  490.7 0.2 copy.41
  490.9 0.0 copy-start.1
  490.9 0.3 copy.64
  491.2 2.3 copy-done.3
  493.5 12.7 %fusion.37 = f32[3,184,1472]{2,1,0:T(8,128)} fusion(f32[1536,1024]{1,0:T(8,128)S(1)} %copy-done.3, f32[3,1024,192]{1,2,0:T(8,128)S(1)} %bitcast.56), kind=kOutput, calls=%fused_computation.41 | convolution fusion | flops 9986048000 | bytes 11540480 | tf_op jit(solution)/shard_map/icr,cn->irn/dot_general | solution.py:137
  506.2 0.0 copy-done.1
  (14 shorter events, 0.2 us)
Async XLA Ops:
  6.5 263.4 %copy-start = (f32[12,12]{1,0:T(8,128)S(1)}, f32[12,12]{1,0:T(8,128)}, u32[]{:S(2)}) copy-start(f32[12,12]{1,0:T(8,128)} %param.5) | copy-start | bytes 1732
  6.5 80.1 %copy-start.4 = (f32[3,184,1472]{2,1,0:T(8,128)S(1)}, f32[3,184,1472]{2,1,0:T(8,128)}, u32[]{:S(2)}) copy-start(f32[3,184,1472]{2,1,0:T(8,128)} %param.4) | copy-start | bytes 9750532
  6.5 76.5 %all-reduce.3.cloned.1.call-start = ((), (), s32[]{:S(2)}) async-start(), calls=%async_computation.5 | async-start | bytes 147456 | tf_op jit(solution)/shard_map/psum | solution.py:15
  128.7 96.2 %all-to-all-start = ((f32[3,192,1024]{1,0,2:T(4,128)}), f32[3,192,1024]{1,0,2:T(4,128)}, u32[]{:S(2)}, u32[]{:S(2)}) async-start(f32[3,192,1024]{1,0,2:T(4,128)} %copy.32), calls=%async_computation | async-start | bytes 8388608 | tf_op jit(solution)/shard_map/all_to_all | solution.py:111
  133.5 208.2 %reduce-scatter.2.cloned.1.call-start = ((), (), s32[]{:S(2)}) async-start(), calls=%async_computation.3 | async-start | bytes 7864320 | tf_op jit(solution)/shard_map/reduce_scatter | solution.py:117
  283.6 0.7 copy-start.5
  283.6 107.5 %all-gather.2.cloned.1.call-start = ((), (), s32[]{:S(2)}) async-start(), calls=%async_computation.4 | async-start | bytes 7864320 | tf_op jit(solution)/shard_map/all_gather | solution.py:133
  391.2 11.4 %copy-start.2 = (f32[1024,1536,1]{1,0,2:T(8,128)S(1)}, f32[1024,1536,1]{1,0,2:T(8,128)}, u32[]{:S(2)}) copy-start(f32[1024,1536,1]{1,0,2:T(8,128)} %fusion.122) | copy-start | bytes 18874372
  413.9 76.8 %all-to-all-start.1 = ((f32[3,128,1536]{1,0,2:T(4,128)}), f32[3,128,1536]{1,0,2:T(4,128)S(1)}, u32[]{:S(2)}, u32[]{:S(2)}) async-start(f32[3,128,1536]{1,0,2:T(4,128)} %copy.40), calls=%async_computation.2 | async-start | bytes 6291456 | tf_op jit(solution)/shard_map/all_to_all | solution.py:139
  490.7 2.8 copy-start.3
  490.9 15.3 %copy-start.1 = (f32[12,12]{1,0:T(8,128)S(1)}, f32[12,12]{1,0:T(8,128)}, u32[]{:S(2)}) copy-start(f32[12,12]{1,0:T(8,128)} %param.5) | copy-start | bytes 1732
Sparse Core Ops, SparseCore 0:
  10.8 72.1 all-reduce.2
  283.8 57.8 reduce-scatter.1
  344.8 46.3 all-gather.1
where the time goes:
time: 522 us; the launch traced here: 513 us
  waiting for transfers between devices  286 us (55%)
  matrix products  120 us (23%)
  other arithmetic  64.1 us (12%)
  local copies, waits for them, and re-layouts  19 us (4%)
  between operations  13.7 us (3%)
  starting transfers between devices  10.6 us (2%)
    all_to_all x1, waiting for transfers between devices, shards(): lax.all_to_all(spec_x, 'wide', split_axis=2, concat_axis=1, tiled=True)  91.4 us
    psum x1, waiting for transfers between devices, spread(): return lax.psum(block, axis)  74.6 us
    reduce_scatter x1, waiting for transfers between devices, shards(): lax.psum_scatter(jnp.einsum('ml,lck->mck', sub_block, spectrum, precision...  56.9 us
    all_to_all x1, waiting for transfers between devices, shards(): lax.all_to_all(rows_back, 'wide', split_axis=2, concat_axis=1, tiled=True)  43.9 us
    dot_general x1, matrix products, shards(): jnp.einsum('irc,rk->ick', lax.all_to_all(spec_x, 'wide', split_axis=2, co...  41.6 us
    dot_general x1, matrix products, shards(): spec_x = jnp.einsum('irn,nc->irc', widened, forward_x, precision=highest)  38.5 us
    dot_general x1, other arithmetic, shards(): jnp.einsum('ick,kr->icr', mixed_levels, inverse_y, precision=highest)  27.9 us
    mul x1, other arithmetic, shards(): forward_x = cas_table(positions, waves, length) * live_mask[None, :]  27.2 us
  transfers between devices with their start and end apart: 5, of which 5 were waited for; matrix products, arithmetic and copies ran while one was open for 11% of the time, Pallas kernels for 0%

commit v1 on v0

--- a/solution.py
+++ b/solution.py
@@ -12,7 +12,7 @@
 
 def spread(block, axis, owner):
     block = jnp.where(lax.axis_index(axis) == owner, block, jnp.zeros_like(block))
-    return lax.psum(block, axis)
+    return jnp.sum(lax.all_gather(block, axis), axis=0)
 
 
 def blend_weights(fraction):

time: 522 us -> 500 us (0.958); the launches traced: 513 us -> 497 us
  waiting for transfers between devices: 286 us -> 200 us
  blocking collectives: 0 us -> 67.4 us
    psum x1 -> x0, waiting for transfers between devices: 74.6 us -> none  [spread(): return lax.psum(block, axis)]
    all_gather x0 -> x2, blocking collectives: none -> 67.4 us  [spread(): return jnp.sum(lax.all_gather(block, axis), axis=0)]
    all_to_all x1, waiting for transfers between devices: 91.4 us -> 80.6 us  [shards(): lax.all_to_all(spec_x, 'wide', split_axis=2, concat_axis=1, tiled=True)]
  transfers between devices with their start and end apart: 5 -> 4, of which waited for: 5 -> 4; matrix products, arithmetic and copies ran while one was open for 11% -> 11% of each run, Pallas kernels for 0% -> 0%
where the time goes in v1:
time: 500 us; the launch traced here: 497 us
  waiting for transfers between devices  200 us (40%)
  matrix products  120 us (24%)
  blocking collectives  67.4 us (13%)
  other arithmetic  64.7 us (13%)
  local copies, waits for them, and re-layouts  19.2 us (4%)
  between operations  13.9 us (3%)
  starting transfers between devices  11.5 us (2%)
    all_to_all x1, waiting for transfers between devices, shards(): lax.all_to_all(spec_x, 'wide', split_axis=2, concat_axis=1, tiled=True)  80.6 us
    all_gather x2, blocking collectives, spread(): return jnp.sum(lax.all_gather(block, axis), axis=0)  67.4 us
    reduce_scatter x1, waiting for transfers between devices, shards(): lax.psum_scatter(jnp.einsum('ml,lck->mck', sub_block, spectrum, precision...  56.7 us
    all_to_all x1, waiting for transfers between devices, shards(): lax.all_to_all(rows_back, 'wide', split_axis=2, concat_axis=1, tiled=True)  43.9 us
    dot_general x1, matrix products, shards(): jnp.einsum('irc,rk->ick', lax.all_to_all(spec_x, 'wide', split_axis=2, co...  41.6 us
    dot_general x1, matrix products, shards(): spec_x = jnp.einsum('irn,nc->irc', widened, forward_x, precision=highest)  38.7 us
    dot_general x1, other arithmetic, shards(): jnp.einsum('ick,kr->icr', mixed_levels, inverse_y, precision=highest)  27.9 us
    mul x1, other arithmetic, shards(): forward_x = cas_table(positions, waves, length) * live_mask[None, :]  27.2 us
  transfers between devices with their start and end apart: 4, of which 4 were waited for; matrix products, arithmetic and copies ran while one was open for 11% of the time, Pallas kernels for 0%

profile of v1, /device:TPU:0, one launch (start us, length us, event | category | flops | bytes accessed | tf_op | source)
XLA Modules:
  0.0 496.9 jit_solution(11500988414860721161)
XLA Ops:
  6.5 0.0 copy-start
  6.5 0.0 copy-start.4
  6.6 1.2 slice_select_fusion.1
  7.8 34.6 %all-gather.1 = f32[24,2,1472]{2,1,0:T(2,128)} all-gather(f32[3,2,1472]{2,1,0:T(2,128)S(1)} %get-tuple-element.10), channel_id=3, replica_groups=mesh['wide'=8,'lev'=4] {'wide'}, dimensions={0}, use_global_device_ids=true | all-gather | bytes 317952 | tf_op jit(solution)/shard_map/all_gather | solution.py:15
  42.4 1.1 reduce_sum.19
  43.5 32.8 %all-gather = f32[24,2,1472]{2,1,0:T(2,128)} all-gather(f32[3,2,1472]{2,1,0:T(2,128)S(1)} %get-tuple-element.9), channel_id=2, replica_groups=mesh['wide'=8,'lev'=4] {'wide'}, dimensions={0}, use_global_device_ids=true | all-gather | bytes 317952 | tf_op jit(solution)/shard_map/all_gather | solution.py:15
  76.3 1.1 reduce_sum.18
  77.5 0.1 multiply_add_fusion.1
  77.6 2.0 fusion.66
  79.6 0.4 multiply_add_fusion
  80.0 0.0 copy-done.4
  80.0 0.4 fusion.124
  80.4 38.7 %fusion.12 = f32[3,192,1024]{2,1,0:T(8,128)S(1)} fusion(f32[1024]{0:T(1024)S(1)} %fusion.85, s32[1024]{0:T(1024)S(1)} %fusion.86, f32[3,192,1536]{2,1,0:T(8,128)S(1)} %fusion.124), kind=kOutput, calls=%fused_computation.15 | convolution fusion | flops 10888937472 | bytes 5906432 | tf_op jit(solution)/shard_map/irn,nc->irc/dot_general | solution.py:108
  119.1 3.2 copy.32
  122.2 5.7 %all-to-all-start = ((f32[3,192,1024]{1,0,2:T(4,128)}), f32[3,192,1024]{1,0,2:T(4,128)}, u32[]{:S(2)}, u32[]{:S(2)}) async-start(f32[3,192,1024]{1,0,2:T(4,128)} %copy.32), calls=%async_computation | async-start | bytes 8388608 | tf_op jit(solution)/shard_map/all_to_all | solution.py:111
  127.9 0.0 reduce-scatter.2.cloned.1.call-start
  128.0 80.6 %all-to-all-done = f32[3,192,1024]{1,0,2:T(4,128)} async-done(((f32[3,192,1024]{1,0,2:T(4,128)}), f32[3,192,1024]{1,0,2:T(4,128)}, u32[]{:S(2)}, u32[]{:S(2)}) %all-to-all-start) | async-done | bytes 2359328 | tf_op jit(solution)/shard_map/all_to_all | solution.py:111
  208.6 3.6 copy.45
  212.2 41.6 %fusion.10 = f32[3,128,1024]{2,1,0:T(8,128)S(1)} fusion(f32[3,1536,128]{2,1,0:T(8,128)S(1)} %bitcast.55, s32[1536]{0:T(1024)S(1)} %fusion.78, f32[1024]{0:T(1024)S(1)} %fusion.85, s32[1024]{0:T(1024)S(1)} %fusion.86), kind=kOutput, calls=%fused_computation.13 | convolution fusion | flops 7265058816 | bytes 3946496 | tf_op jit(solution)/shard_map/irc,rk->ick/dot_general | solution.py:109
  253.8 0.0 copy-done
  253.8 7.3 %fusion.59 = f32[12,128,1024]{2,0,1:T(8,128)S(1)} fusion(f32[3,128,1024]{2,1,0:T(8,128)S(1)} %fusion.10, f32[12,12]{1,0:T(8,128)S(1)} %copy-done, s32[]{:T(128)S(6)} %select_n.144), kind=kOutput, calls=%fused_computation.63 | convolution fusion | flops 56623104 | bytes 7864900 | tf_op jit(solution)/shard_map/ml,lck->mck/dot_general | solution.py:118
  261.2 6.3 %copy.37 = f32[12,128,1024]{2,1,0:T(8,128)} copy(f32[12,128,1024]{2,0,1:T(8,128)S(1)} %fusion.59) | data formatting | bytes 12582912 | tf_op jit(solution)/shard_map/ml,lck->mck/dot_general | solution.py:118
  267.4 0.0 copy-start.5
  267.4 0.0 reduce-scatter.2.cloned.1.call-update
  267.5 0.0 all-gather.4.cloned.1.call-start
  267.5 0.1 dynamic_slice.21
  267.6 0.1 dynamic_slice.23
  267.7 0.4 copy-done.5
  268.1 0.1 dynamic_slice.22
  268.2 0.1 dynamic-slice_multiply_fusion
  268.3 0.1 broadcast_add_fusion
  268.4 0.2 multiply_select_fusion
  268.6 56.7 %reduce-scatter.2.cloned.1.call-done = f32[3,128,1024]{2,1,0:T(8,128)} async-done(((f32[12,128,1024]{2,1,0:T(8,128)}), f32[3,128,1024]{2,1,0:T(8,128)}) %reduce-scatter.2.cloned.1.call-update) | async-done | bytes 1572880 | tf_op jit(solution)/shard_map/reduce_scatter | solution.py:117
  325.3 2.9 add_divide_fusion
  328.3 0.0 all-gather.4.cloned.1.call-update
  328.3 27.9 %fusion.122 = f32[1024,1536,1]{1,0,2:T(8,128)} fusion(f32[1024]{0:T(1024)S(1)} %fusion.85, s32[1024]{0:T(1024)S(1)} %fusion.86, s32[1536]{0:T(1024)S(1)} %fusion.78), kind=kLoop, calls=%fused_computation.12.clone.1 | loop fusion | flops 18874368 | bytes 6305792 | tf_op jit(solution)/shard_map/ick,kr->icr/dot_general | solution.py:136
  356.1 18.7 %all-gather.4.cloned.1.call-done = f32[12,128,1024]{2,1,0:T(8,128)} async-done(((f32[3,128,1024]{2,1,0:T(8,128)}), f32[12,128,1024]{2,1,0:T(8,128)}) %all-gather.4.cloned.1.call-update) | async-done | bytes 6291472 | tf_op jit(solution)/shard_map/all_gather | solution.py:133
  374.8 0.0 copy-start.2
  374.8 11.3 %fusion = f32[3,128,1024]{2,0,1:T(4,128)S(1)} fusion(f32[12,128,1024]{2,1,0:T(8,128)} %all-gather.4.cloned.1.call-done, f32[12,12]{1,0:T(8,128)} %param.6, s32[]{:T(128)S(6)} %select_n.144), kind=kOutput, calls=%fused_computation.3 | convolution fusion | flops 56623104 | bytes 7866372 | tf_op jit(solution)/shard_map/lm,mck->lck/dot_general | solution.py:135
  386.1 0.0 copy-done.2
  386.2 8.6 %fusion.8 = f32[3,128,1536]{2,1,0:T(8,128)S(1)} fusion(f32[3,128,1024]{2,0,1:T(4,128)S(1)} %fusion, f32[1024,1536,1]{1,0,2:T(8,128)S(1)} %copy-done.2), kind=kOutput, calls=%fused_computation.11 | convolution fusion | flops 7247757312 | bytes 10223616 | tf_op jit(solution)/shard_map/ick,kr->icr/dot_general | solution.py:136
  394.8 2.7 copy.40
  397.5 5.8 %all-to-all-start.1 = ((f32[3,128,1536]{1,0,2:T(4,128)}), f32[3,128,1536]{1,0,2:T(4,128)S(1)}, u32[]{:S(2)}, u32[]{:S(2)}) async-start(f32[3,128,1536]{1,0,2:T(4,128)} %copy.40), calls=%async_computation.2 | async-start | bytes 6291456 | tf_op jit(solution)/shard_map/all_to_all | solution.py:139
  403.3 27.2 %add_multiply_fusion = f32[1536,1024]{1,0:T(8,128)} fusion(f32[1024]{0:T(1024)S(1)} %fusion.85, s32[1024]{0:T(1024)S(1)} %fusion.86), kind=kLoop, calls=%fused_computation.32 | loop fusion | flops 17301504 | bytes 6299648 | tf_op jit(solution)/shard_map/mul | solution.py:94
  430.4 43.9 %all-to-all-done.1 = f32[3,128,1536]{1,0,2:T(4,128)S(1)} async-done(((f32[3,128,1536]{1,0,2:T(4,128)}), f32[3,128,1536]{1,0,2:T(4,128)S(1)}, u32[]{:S(2)}, u32[]{:S(2)}) %all-to-all-start.1) | async-done | bytes 2359328 | tf_op jit(solution)/shard_map/all_to_all | solution.py:139
  474.3 0.0 copy-start.3
  474.3 0.2 copy.41
  474.5 0.0 copy-start.1
  474.5 0.3 copy.64
  474.8 2.3 copy-done.3
  477.1 12.7 %fusion.37 = f32[3,184,1472]{2,1,0:T(8,128)} fusion(f32[1536,1024]{1,0:T(8,128)S(1)} %copy-done.3, f32[3,1024,192]{1,2,0:T(8,128)S(1)} %bitcast.54), kind=kOutput, calls=%fused_computation.41 | convolution fusion | flops 9986048000 | bytes 11540480 | tf_op jit(solution)/shard_map/icr,cn->irn/dot_general | solution.py:137
  489.8 0.0 copy-done.1
  (14 shorter events, 0.2 us)
Async XLA Ops:
  6.5 247.3 %copy-start = (f32[12,12]{1,0:T(8,128)S(1)}, f32[12,12]{1,0:T(8,128)}, u32[]{:S(2)}) copy-start(f32[12,12]{1,0:T(8,128)} %param.5) | copy-start | bytes 1732
  6.5 73.5 %copy-start.4 = (f32[3,184,1472]{2,1,0:T(8,128)S(1)}, f32[3,184,1472]{2,1,0:T(8,128)}, u32[]{:S(2)}) copy-start(f32[3,184,1472]{2,1,0:T(8,128)} %param.4) | copy-start | bytes 9750532
  122.2 86.3 %all-to-all-start = ((f32[3,192,1024]{1,0,2:T(4,128)}), f32[3,192,1024]{1,0,2:T(4,128)}, u32[]{:S(2)}, u32[]{:S(2)}) async-start(f32[3,192,1024]{1,0,2:T(4,128)} %copy.32), calls=%async_computation | async-start | bytes 8388608 | tf_op jit(solution)/shard_map/all_to_all | solution.py:111
  127.9 197.4 %reduce-scatter.2.cloned.1.call-start = ((), (), s32[]{:S(2)}) async-start(), calls=%async_computation.3 | async-start | bytes 7864320 | tf_op jit(solution)/shard_map/reduce_scatter | solution.py:117
  267.4 0.7 copy-start.5
  267.5 107.3 %all-gather.4.cloned.1.call-start = ((), (), s32[]{:S(2)}) async-start(), calls=%async_computation.4 | async-start | bytes 7864320 | tf_op jit(solution)/shard_map/all_gather | solution.py:133
  374.8 11.4 %copy-start.2 = (f32[1024,1536,1]{1,0,2:T(8,128)S(1)}, f32[1024,1536,1]{1,0,2:T(8,128)}, u32[]{:S(2)}) copy-start(f32[1024,1536,1]{1,0,2:T(8,128)} %fusion.122) | copy-start | bytes 18874372
  397.5 76.8 %all-to-all-start.1 = ((f32[3,128,1536]{1,0,2:T(4,128)}), f32[3,128,1536]{1,0,2:T(4,128)S(1)}, u32[]{:S(2)}, u32[]{:S(2)}) async-start(f32[3,128,1536]{1,0,2:T(4,128)} %copy.40), calls=%async_computation.2 | async-start | bytes 6291456 | tf_op jit(solution)/shard_map/all_to_all | solution.py:139
  474.3 2.8 copy-start.3
  474.5 15.3 %copy-start.1 = (f32[12,12]{1,0:T(8,128)S(1)}, f32[12,12]{1,0:T(8,128)}, u32[]{:S(2)}) copy-start(f32[12,12]{1,0:T(8,128)} %param.5) | copy-start | bytes 1732
Sparse Core Ops, SparseCore 0:
  267.6 57.6 reduce-scatter.1
  328.4 46.3 all-gather.3
